TPU v7x, 512 devices: a whole 4x8x8 slice. The times are simulated.
512 devices in a mesh: section: 4 (over x), seq: 8 (over y), dp: 16 (over z, core).
Axes of the slice: x: 4, y: 8, z: 8, core: 2. Of those that a mesh axis runs over, the one named last changes fastest.
Arguments:
- queries: bfloat16 [16, 1024, 32, 128], P('dp', 'seq', 'section'), may hold values from -18 to 18
- video_keys: bfloat16 [16, 1024, 32, 128], P('dp', 'seq', 'section'), may hold values from -18 to 18
- video_values: bfloat16 [16, 1024, 32, 128], P('dp', 'seq', 'section'), may hold values from -6 to 6
- cross_queries: bfloat16 [16, 1024, 32, 128], P('dp', 'seq', 'section'), may hold values from -8 to 8
- self_cotangent: bfloat16 [16, 1024, 32, 128], P('dp', 'seq', 'section'), may hold values from -6 to 6
- cross_cotangent: bfloat16 [16, 1024, 32, 128], P('dp', 'seq', 'section'), may hold values from -6 to 6
- caption_states: bfloat16 [16, 512, 4096], P('dp', 'seq'), may hold values from -400 to 400
- caption_gain: float32 [4096], replicated, may hold values from 0.25 to 1.75
- key_weight: bfloat16 [4096, 4096], P('dp', ('section', 'seq')), may hold values from -0.09375 to 0.09375
- value_weight: bfloat16 [4096, 4096], P('dp', ('section', 'seq')), may hold values from -0.09375 to 0.09375
- video_length: int32 [16], replicated, may hold values from 512 to 1024, as said below
- caption_length: int32 [16], replicated, may hold values from 128 to 512, as said below
Outputs:
- query_gradient: bfloat16 [16, 1024, 32, 128], P('dp', 'seq', 'section')
- key_gradient: bfloat16 [16, 1024, 32, 128], P('dp', 'seq', 'section')
- value_gradient: bfloat16 [16, 1024, 32, 128], P('dp', 'seq', 'section')
- cross_query_gradient: bfloat16 [16, 1024, 32, 128], P('dp', 'seq', 'section')
- key_weight_gradient: float32 [4096, 4096], P('dp', ('section', 'seq'))
- value_weight_gradient: float32 [4096, 4096], P('dp', ('section', 'seq'))
Inputs may be any that keep to these rules, and one draw needn't show every extreme that they name: `video_length`: some clip has all 1024 tokens valid. `caption_length`: some clip has all 512 caption tokens valid.
All inputs are finite; a program needn't handle non-finite values.
Results may differ from a plain program's by a relative error of at most 0.018.
Values may be sent and summed in bfloat16 or wider, within the bound.
A program may use at most 64 MiB of HBM per device.

v0:
```python
import math
import jax
import jax.numpy as jnp
from jax import lax
from jax.sharding import PartitionSpec as P

norm_epsilon = 1e-06


def sent_together(arrays, axis, dim, along):
    ends, at = ([], 0)
    for a in arrays[:-1]:
        at += a.shape[along]
        ends.append(at)
    both = jnp.concatenate(arrays, axis=along)
    return tuple(jnp.split(lax.all_gather(both, axis, axis=dim, tiled=True), ends, axis=along))


def side_by_side(arrays, axis, split_dim, concat_dim, along):
    widths = [a.shape[along] for a in arrays]
    both = jnp.concatenate(arrays, axis=along)
    out = lax.all_to_all(both, axis, split_axis=split_dim, concat_axis=concat_dim, tiled=True)
    return tuple(jnp.split(out, [sum(widths[:k]) for k in range(1, len(widths))], axis=along))


def normalize_rows(states, caption_gain):
    values = states.astype(jnp.float32)
    mean_square = jnp.mean(values * values, axis=-1, keepdims=True)
    return (values * lax.rsqrt(mean_square + norm_epsilon) * caption_gain).astype(jnp.bfloat16)


def block_gradients(query_rows, cotangent_rows, key_rows, value_rows, key_limit, score_scale):
    scores = (
        jnp.einsum("qhd,khd->hqk", query_rows, key_rows, preferred_element_type=jnp.float32)
        * score_scale
    )
    columns = lax.broadcasted_iota(jnp.int32, scores.shape, 2)
    scores = jnp.where(columns < key_limit, scores, -jnp.inf)
    maxima = jnp.max(scores, axis=-1, keepdims=True)
    powers = jnp.exp(scores - maxima)
    weights = powers / jnp.sum(powers, axis=-1, keepdims=True)
    weights_low = weights.astype(jnp.bfloat16)
    weight_grad = jnp.einsum(
        "qhd,khd->hqk", cotangent_rows, value_rows, preferred_element_type=jnp.float32
    )
    row_total = jnp.sum(weights * weight_grad, axis=-1, keepdims=True)
    score_grad = (weights * (weight_grad - row_total) * score_scale).astype(jnp.bfloat16)
    query_grad = jnp.einsum(
        "hqk,khd->qhd", score_grad, key_rows, preferred_element_type=jnp.float32
    )
    key_grad = jnp.einsum(
        "hqk,qhd->khd", score_grad, query_rows, preferred_element_type=jnp.float32
    )
    value_grad = jnp.einsum(
        "hqk,qhd->khd", weights_low, cotangent_rows, preferred_element_type=jnp.float32
    )
    return (query_grad, key_grad, value_grad)


def attention_gradients(query_set, cotangent_set, key_set, value_set, key_limit, score_scale):
    row_count = query_set.shape[0]
    block_rows = math.gcd(row_count, 512)
    block_count = row_count // block_rows
    query_blocks = query_set.reshape((block_count, block_rows) + query_set.shape[1:])
    cotangent_blocks = cotangent_set.reshape((block_count, block_rows) + cotangent_set.shape[1:])

    def advance(totals, inputs):
        query_grad, key_grad, value_grad = block_gradients(
            inputs[0], inputs[1], key_set, value_set, key_limit, score_scale
        )
        return ((totals[0] + key_grad, totals[1] + value_grad), query_grad)

    empty = jnp.zeros(key_set.shape, jnp.float32)
    totals, query_grads = lax.scan(advance, (empty, empty), (query_blocks, cotangent_blocks))
    return (query_grads.reshape(query_set.shape), totals[0], totals[1])


def local(
    queries,
    video_keys,
    video_values,
    cross_queries,
    self_cotangent,
    cross_cotangent,
    caption_states,
    caption_gain,
    key_weight,
    value_weight,
    video_length,
    caption_length,
):
    head_size = queries.shape[3]
    score_scale = 1.0 / math.sqrt(head_size)
    head_width = key_weight.shape[1]
    local_heads = head_width // head_size
    normed = normalize_rows(lax.all_gather(caption_states, "seq", axis=1, tiled=True), caption_gain)
    normed_text = normed[0]
    caption_rows = normed_text.shape[0]
    pieces = sent_together((key_weight, value_weight), "dp", 0, 1)
    columns = normed_text
    text_keys = jnp.dot(columns, pieces[0], preferred_element_type=jnp.float32)
    text_values = jnp.dot(columns, pieces[1], preferred_element_type=jnp.float32)
    text_keys = text_keys.astype(jnp.bfloat16).reshape(caption_rows, local_heads, head_size)
    text_values = text_values.astype(jnp.bfloat16).reshape(caption_rows, local_heads, head_size)
    gathered = side_by_side(
        (queries, video_keys, video_values, cross_queries, self_cotangent, cross_cotangent),
        "seq",
        2,
        1,
        0,
    )
    head_queries, head_keys, head_values, head_cross, self_rows, cross_rows = (
        tensor[0] for tensor in gathered
    )
    clip_index = lax.axis_index("dp")
    video_limit = lax.dynamic_index_in_dim(video_length, clip_index, 0, keepdims=False)
    caption_limit = lax.dynamic_index_in_dim(caption_length, clip_index, 0, keepdims=False)
    positions = lax.broadcasted_iota(jnp.int32, (head_queries.shape[0], 1, 1), 0)
    nothing = jnp.zeros((), jnp.bfloat16)
    self_rows = jnp.where(positions < video_limit, self_rows, nothing)
    cross_rows = jnp.where(positions < video_limit, cross_rows, nothing)
    query_grad, key_grad, value_grad = attention_gradients(
        head_queries, self_rows, head_keys, head_values, video_limit, score_scale
    )
    cross_grad, text_key_grad, text_value_grad = attention_gradients(
        head_cross, cross_rows, text_keys, text_values, caption_limit, score_scale
    )
    returned = side_by_side(
        (
            query_grad.astype(jnp.bfloat16)[None],
            key_grad.astype(jnp.bfloat16)[None],
            value_grad.astype(jnp.bfloat16)[None],
            cross_grad.astype(jnp.bfloat16)[None],
        ),
        "seq",
        1,
        2,
        0,
    )
    key_cot = text_key_grad.astype(jnp.bfloat16).reshape(caption_rows, head_width)
    value_cot = text_value_grad.astype(jnp.bfloat16).reshape(caption_rows, head_width)
    stacked = jnp.concatenate((key_cot, value_cot), axis=1)
    contract_rows = (((0,), (0,)), ((), ()))
    columns = normed_text
    gradients = lax.psum_scatter(
        lax.dot_general(columns, stacked, contract_rows, preferred_element_type=jnp.float32).astype(
            jnp.bfloat16
        ),
        "dp",
        scatter_dimension=0,
        tiled=True,
    ).astype(jnp.float32)
    return (
        returned[0],
        returned[1],
        returned[2],
        returned[3],
        gradients[:, :head_width],
        gradients[:, head_width:],
    )


def solution(mesh):
    placed = (
        P("dp", "seq", "section", None),
        P("dp", "seq", "section", None),
        P("dp", "seq", "section", None),
        P("dp", "seq", "section", None),
        P("dp", "seq", "section", None),
        P("dp", "seq", "section", None),
        P("dp", "seq", None),
        P(),
        P("dp", ("section", "seq")),
        P("dp", ("section", "seq")),
        P(),
        P(),
    )
    return jax.shard_map(
        local,
        mesh=mesh,
        in_specs=placed,
        out_specs=(
            P("dp", "seq", "section", None),
            P("dp", "seq", "section", None),
            P("dp", "seq", "section", None),
            P("dp", "seq", "section", None),
            P("dp", ("section", "seq")),
            P("dp", ("section", "seq")),
        ),
        check_vma=False,
    )
```

profile of v0, /device:TPU:12, one launch (start us, length us, event | category | flops | bytes accessed | tf_op | source)
XLA Modules:
  0.0 239.1 jit_solution(1283080764883097908)
XLA Ops:
  8.0 1.5 pad_maximum_fusion.1
  9.6 1.7 copy_dynamic-update-slice_fusion.5
  11.3 1.7 copy_dynamic-update-slice_fusion.4
  16.1 7.5 %all-to-all-start = ((bf16[6,128,8,128]{3,1,0,2:T(8,128)(2,1)}), bf16[6,128,8,128]{3,1,0,2:T(8,128)(2,1)S(1)}, u32[]{:S(2)}, u32[]{:S(2)}) async-start(bf16[6,128,8,128]{3,1,0,2:T(8,128)(2,1)} %copy_dynamic-update-slice_fusion), calls=%async_computation | async-start | bytes 3145728 | tf_op jit(solution)/shard_map/all_to_all | solution.py:22
  25.5 50.6 %all-to-all-done = bf16[6,128,8,128]{3,1,0,2:T(8,128)(2,1)S(1)} async-done(((bf16[6,128,8,128]{3,1,0,2:T(8,128)(2,1)}), bf16[6,128,8,128]{3,1,0,2:T(8,128)(2,1)S(1)}, u32[]{:S(2)}, u32[]{:S(2)}) %all-to-all-start) | async-done | bytes 1572896 | tf_op jit(solution)/shard_map/all_to_all | solution.py:22
  77.1 0.9 select_bitcast_fusion.1
  78.0 21.0 %all-gather.3.cloned.1.call-done = bf16[1,512,4096]{2,1,0:T(8,128)(2,1)} async-done(((bf16[1,64,4096]{2,1,0:T(8,128)(2,1)}), bf16[1,512,4096]{2,1,0:T(8,128)(2,1)}) %all-gather.3.cloned.1.call-update) | async-done | bytes 4194320 | tf_op jit(solution)/shard_map/all_gather | solution.py:96
  99.0 3.1 %fusion.49 = f32[512]{0:T(512)S(1)} fusion(bf16[1,512,4096]{2,1,0:T(8,128)(2,1)} %all-gather.3.cloned.1.call-done), kind=kLoop, calls=%fused_computation.65 | loop fusion | flops 6290944 | bytes 4196352 | tf_op jit(solution)/shard_map/reduce_sum | solution.py:28
  102.1 45.8 %all-gather.5.cloned.1.call-done = bf16[4096,256]{1,0:T(8,128)(2,1)} async-done(((bf16[256,256]{1,0:T(8,128)(2,1)}), bf16[4096,256]{1,0:T(8,128)(2,1)}) %all-gather.5.cloned.1.call-update) | async-done | bytes 2097168 | tf_op jit(solution)/shard_map/all_gather | solution.py:16
  147.9 3.9 %fusion.53 = bf16[512,1,128]{2,0,1:T(8,128)(2,1)S(1)} fusion(bf16[4096,256]{1,0:T(8,128)(2,1)} %all-gather.5.cloned.1.call-done, bf16[1,512,4096]{2,1,0:T(8,128)(2,1)} %all-gather.3.cloned.1.call-done, f32[4096]{0:T(1024)S(1)} %copy-done.9, f32[512]{0:T(512)S(1)} %add_rsqrt_fusion), kind=kOutput, calls=%fused_computation.73 | convolution fusion | flops 545325056 | bytes 5392384 | tf_op jit(solution)/shard_map/dot_general | solution.py:101
  152.4 1.3 fusion.54
  153.7 8.4 %while.31 = (s32[]{:T(128)}, f32[512,1,128]{0,2,1:T(8,128)}, f32[512,1,128]{0,2,1:T(8,128)S(1)}, bf16[2,512,1,128]{3,1,2,0:T(8,128)(2,1)S(1)}, bf16[2,512,1,128]...) while((s32[]{:T(128)}, f32[512,1,128]{0,2,1:T(8,128)}, ...), condition=%wide.region_10.11_spmd.clone, body=%wide.region_6.10_spmd.clone.sunk | while | flops 340524032 | bytes 11164816 | solution.py:74
  156.1 1.0 fusion.112
  159.8 2.0 fusion.112
  162.2 1.1 convert_bitcast_fusion.2
  163.3 5.2 %convolution_convert_fusion = bf16[4096,256]{1,0:T(8,128)(2,1)} fusion(bf16[512,128]{0,1:T(8,128)(2,1)S(1)} %get-tuple-element.309, bf16[512,128]{0,1:T(8,128)(2,1)S(1)} %get-tuple-element.310, bf16[1,512,4096]{2,1,0:T(8,128)(2,1)} %all-gather.3.cloned.1.call-done, f32[4096]{0:T(1024)S(1)} %copy-done.9, f32[512]{0:T(512)S(1)} %add_rsqrt_fusion), kind=kOutput, calls=%fused_computation.68 | convolution fusion | flops 1083703296 | bytes 6572032 | tf_op jit(solution)/shard_map/dot_general | solution.py:146
  168.6 13.7 %while.30 = (s32[]{:T(128)}, f32[1024,1,128]{0,2,1:T(8,128)S(1)}, f32[1024,1,128]{0,2,1:T(8,128)}, bf16[2,512,1,128]{3,1,2,0:T(8,128)(2,1)S(1)}, bf16[2,512,1,12...) while((s32[]{:T(128)}, f32[1024,1,128]{0,2,1:T(8,128)S(1)}, ...), condition=%wide.region_4.5_spmd.clone, body=%wide.region_0.4_spmd.clone.sunk | while | flops 685243904 | bytes 23622340 | solution.py:74
  170.4 2.6 %fusion.102 = f32[1024,1,128]{0,2,1:T(8,128)} fusion(f32[1024,1,128]{0,2,1:T(8,128)} %get-tuple-element.483, pred[]{:T(512)S(6)} %compare.6, bf16[2,512,1,128]{3,1,2,0:T(8,128)(2,1)} %get-tuple-element.499, s32[]{:T(128)} %get-tuple-element.481, f32[512,1024]{1,0:T(8,128)S(1)} %get-tuple-element.420, f32[512]{0:T(512)S(1)} %fusion.100, ...), kind=kOutput, calls=%fused_computation.10.clone.1 | convolution fusion | flops 137101312 | bytes 3282433 | tf_op jit(solution)/shard_map/while/body/eval_jaxpr/hqk,qhd->khd/dot_general | solution.py:54
  177.1 2.8 %fusion.102 = f32[1024,1,128]{0,2,1:T(8,128)} fusion(f32[1024,1,128]{0,2,1:T(8,128)} %get-tuple-element.483, pred[]{:T(512)S(6)} %compare.6, bf16[2,512,1,128]{3,1,2,0:T(8,128)(2,1)} %get-tuple-element.499, s32[]{:T(128)} %get-tuple-element.481, f32[512,1024]{1,0:T(8,128)S(1)} %get-tuple-element.420, f32[512]{0:T(512)S(1)} %fusion.100, ...), kind=kOutput, calls=%fused_computation.10.clone.1 | convolution fusion | flops 137101312 | bytes 3282433 | tf_op jit(solution)/shard_map/while/body/eval_jaxpr/hqk,qhd->khd/dot_general | solution.py:54
  182.3 1.2 copy.73
  183.7 1.1 pad_maximum_fusion
  185.6 34.7 %all_to_all.30 = bf16[4,1024,1,128]{3,0,2,1:T(4,128)(2,1)S(1)} all-to-all(bf16[4,1024,1,128]{3,0,2,1:T(4,128)(2,1)S(1)} %copy.77), channel_id=1, replica_groups=mesh['section'=4,'seq'=8,'dp'=16] {'seq'}, dimensions={1} | all-to-all | bytes 2097152 | tf_op jit(solution)/shard_map/all_to_all | solution.py:22
  224.0 6.9 %reduce-scatter.2.cloned.1.call-done = bf16[256,256]{1,0:T(8,128)(2,1)} async-done(((bf16[4096,256]{1,0:T(8,128)(2,1)}), bf16[256,256]{1,0:T(8,128)(2,1)}) %reduce-scatter.2.cloned.1.call-update) | async-done | bytes 131088 | tf_op jit(solution)/shard_map/reduce_scatter | solution.py:145
  230.9 1.6 fusion.66
  (86 shorter events, 25.4 us)
Async XLA Ops:
  7.2 5.8 %copy-start.3 = (bf16[1,128,8,128]{3,2,1,0:T(8,128)(2,1)S(1)}, bf16[1,128,8,128]{3,2,1,0:T(8,128)(2,1)}, u32[]{:S(2)}) copy-start(bf16[1,128,8,128]{3,2,1,0:T(8,128)(2,1)} %param.18) | copy-start | bytes 786436
  7.2 6.6 %copy-start.4 = (bf16[1,128,8,128]{3,2,1,0:T(8,128)(2,1)S(1)}, bf16[1,128,8,128]{3,2,1,0:T(8,128)(2,1)}, u32[]{:S(2)}) copy-start(bf16[1,128,8,128]{3,2,1,0:T(8,128)(2,1)} %param.19) | copy-start | bytes 786436
  7.2 7.3 %copy-start.5 = (bf16[1,128,8,128]{3,2,1,0:T(8,128)(2,1)S(1)}, bf16[1,128,8,128]{3,2,1,0:T(8,128)(2,1)}, u32[]{:S(2)}) copy-start(bf16[1,128,8,128]{3,2,1,0:T(8,128)(2,1)} %param.20) | copy-start | bytes 786436
  7.2 8.1 %copy-start.6 = (bf16[1,128,8,128]{3,2,1,0:T(8,128)(2,1)S(1)}, bf16[1,128,8,128]{3,2,1,0:T(8,128)(2,1)}, u32[]{:S(2)}) copy-start(bf16[1,128,8,128]{3,2,1,0:T(8,128)(2,1)} %param.21) | copy-start | bytes 786436
  7.2 91.8 %all-gather.3.cloned.1.call-start = ((), (), s32[]{:S(2)}) async-start(), calls=%async_computation.3 | async-start | bytes 4718592 | tf_op jit(solution)/shard_map/all_gather | solution.py:96
  7.9 140.0 %all-gather.5.cloned.1.call-start = ((), (), s32[]{:S(2)}) async-start(), calls=%async_computation.4 | async-start | bytes 2228224 | tf_op jit(solution)/shard_map/all_gather | solution.py:16
  14.5 9.1 %copy-start.10 = (s32[16]{0:T(128)S(1)}, s32[16]{0:T(128)}, u32[]{:S(2)}) copy-start(s32[16]{0:T(128)} %param.26) | copy-start | bytes 196
  14.5 9.8 %copy-start.11 = (s32[16]{0:T(128)S(1)}, s32[16]{0:T(128)}, u32[]{:S(2)}) copy-start(s32[16]{0:T(128)} %param.27) | copy-start | bytes 196
  16.1 60.0 %all-to-all-start = ((bf16[6,128,8,128]{3,1,0,2:T(8,128)(2,1)}), bf16[6,128,8,128]{3,1,0,2:T(8,128)(2,1)S(1)}, u32[]{:S(2)}, u32[]{:S(2)}) async-start(bf16[6,128,8,128]{3,1,0,2:T(8,128)(2,1)} %copy_dynamic-update-slice_fusion), calls=%async_computation | async-start | bytes 3145728 | tf_op jit(solution)/shard_map/all_to_all | solution.py:22
  23.6 207.3 %reduce-scatter.2.cloned.1.call-start = ((), (), s32[]{:S(2)}) async-start(), calls=%async_computation.5 | async-start | bytes 2228224 | tf_op jit(solution)/shard_map/reduce_scatter | solution.py:145
  78.0 70.0 %copy-start.9 = (f32[4096]{0:T(1024)S(1)}, f32[4096]{0:T(1024)}, u32[]{:S(2)}) copy-start(f32[4096]{0:T(1024)} %param.23) | copy-start | bytes 49156
  147.9 4.0 %copy-start = (bf16[1,512,4096]{2,1,0:T(8,128)(2,1)S(1)}, bf16[1,512,4096]{2,1,0:T(8,128)(2,1)}, u32[]{:S(2)}) copy-start(bf16[1,512,4096]{2,1,0:T(8,128)(2,1)} %all-gather.3.cloned.1.call-done) | copy-start | bytes 12582916
  147.9 4.4 %copy-start.8 = (bf16[4096,256]{1,0:T(8,128)(2,1)S(1)}, bf16[4096,256]{1,0:T(8,128)(2,1)}, u32[]{:S(2)}) copy-start(bf16[4096,256]{1,0:T(8,128)(2,1)} %all-gather.5.cloned.1.call-done) | copy-start | bytes 6291460
  162.2 6.3 %copy-start.1 = (bf16[2,512,1,128]{3,1,2,0:T(8,128)(2,1)}, bf16[2,512,1,128]{3,1,2,0:T(8,128)(2,1)S(1)}, u32[]{:S(2)}) copy-start(bf16[2,512,1,128]{3,1,2,0:T(8,128)(2,1)S(1)} %get-tuple-element.107) | copy-start | bytes 786436
  170.3 2.6 %copy-start.2 = (bf16[1024,1,128]{2,0,1:T(8,128)(2,1)S(1)}, bf16[1024,1,128]{2,0,1:T(8,128)(2,1)}, u32[]{:S(2)}) copy-start(bf16[1024,1,128]{2,0,1:T(8,128)(2,1)} %get-tuple-element.500) | copy-start | bytes 786436 | tf_op jit(solution)/shard_map/while
  170.3 2.6 %copy-start.7 = (bf16[2,512,1,128]{3,1,2,0:T(8,128)(2,1)S(1)}, bf16[2,512,1,128]{3,1,2,0:T(8,128)(2,1)}, u32[]{:S(2)}) copy-start(bf16[2,512,1,128]{3,1,2,0:T(8,128)(2,1)} %get-tuple-element.499) | copy-start | bytes 786436 | tf_op jit(solution)/shard_map/while
  177.1 2.8 %copy-start.2 = (bf16[1024,1,128]{2,0,1:T(8,128)(2,1)S(1)}, bf16[1024,1,128]{2,0,1:T(8,128)(2,1)}, u32[]{:S(2)}) copy-start(bf16[1024,1,128]{2,0,1:T(8,128)(2,1)} %get-tuple-element.500) | copy-start | bytes 786436 | tf_op jit(solution)/shard_map/while
  177.1 2.8 %copy-start.7 = (bf16[2,512,1,128]{3,1,2,0:T(8,128)(2,1)S(1)}, bf16[2,512,1,128]{3,1,2,0:T(8,128)(2,1)}, u32[]{:S(2)}) copy-start(bf16[2,512,1,128]{3,1,2,0:T(8,128)(2,1)} %get-tuple-element.499) | copy-start | bytes 786436 | tf_op jit(solution)/shard_map/while
Sparse Core Ops, SparseCore 0:
  10.1 88.8 all-gather.2
  101.7 46.1 all-gather.4
  168.7 62.2 reduce-scatter.1
where the time goes:
time: 240 us; the launch traced here: 239 us
  waiting for transfers between devices  125 us (52%)
  blocking collectives  34.7 us (14%)
  matrix products  26 us (11%)
  local copies, waits for them, and re-layouts  16.8 us (7%)
  other arithmetic  14.5 us (6%)
  between operations  13.9 us (6%)
  starting transfers between devices  7.62 us (3%)
    all_to_all x1, waiting for transfers between devices, side_by_side(): lax.all_to_all(both, axis, split_axis=split_dim, concat_axis=concat_dim,...  50.6 us
    all_gather x1, waiting for transfers between devices, sent_together(): lax.all_gather(both, axis, axis=dim, tiled=True)  45.8 us
    all_to_all x1, blocking collectives, side_by_side(): lax.all_to_all(both, axis, split_axis=split_dim, concat_axis=concat_dim,...  34.7 us
    all_gather x1, waiting for transfers between devices, local(): lax.all_gather(caption_states, 'seq', axis=1, tiled=True)  21 us
    unnamed x29, local copies, waits for them, and re-layouts  9.77 us
    all_to_all x1, starting transfers between devices, side_by_side(): lax.all_to_all(both, axis, split_axis=split_dim, concat_axis=concat_dim,...  7.55 us
    reduce_scatter x1, waiting for transfers between devices, local(): lax.psum_scatter(lax.dot_general(columns, stacked, contract_rows, preferr...  6.91 us
    dot_general x4, matrix products, block_gradients(): jnp.einsum('hqk,qhd->khd', weights_low, cotangent_rows, preferred_element...  6.08 us
  transfers between devices with their start and end apart: 4, of which 4 were waited for; matrix products, arithmetic and copies ran while one was open for 15% of the time, Pallas kernels for 0%

commit v1 on v0

--- a/solution.py
+++ b/solution.py
@@ -5,6 +5,28 @@
 from jax.sharding import PartitionSpec as P
 
 norm_epsilon = 1e-06
+
+
+def joined_along(blocks, dim):
+    lengths = list(blocks.shape[1:])
+    lengths[dim] *= blocks.shape[0]
+    return jnp.moveaxis(blocks, 0, dim).reshape(lengths)
+
+
+def ring_gather(value, axis, dim):
+    size = lax.axis_size(axis)
+    pairs = [(i, (i + 1) % size) for i in range(size)]
+    back = [(b, a) for a, b in pairs]
+    lower, upper = ([], [])
+    for step in range(size - 1):
+        if step % 2 == 0:
+            lower.append(lax.ppermute(lower[-1] if lower else value, axis, pairs))
+        else:
+            upper.append(lax.ppermute(upper[-1] if upper else value, axis, back))
+    parts = jnp.stack([*lower[::-1], value, *upper])
+    shift = lax.axis_index(axis) - len(lower)
+    parts = parts[(jnp.arange(size) - shift) % size]
+    return joined_along(parts, dim)
 
 
 def sent_together(arrays, axis, dim, along):
@@ -93,7 +115,7 @@
     score_scale = 1.0 / math.sqrt(head_size)
     head_width = key_weight.shape[1]
     local_heads = head_width // head_size
-    normed = normalize_rows(lax.all_gather(caption_states, "seq", axis=1, tiled=True), caption_gain)
+    normed = normalize_rows(ring_gather(caption_states, "seq", 1), caption_gain)
     normed_text = normed[0]
     caption_rows = normed_text.shape[0]
     pieces = sent_together((key_weight, value_weight), "dp", 0, 1)

time: 240 us -> 223 us (0.929)
  waiting for transfers between devices: 125 us -> 69.1 us
  starting transfers between devices: 7.62 us -> 29.8 us
  local copies, waits for them, and re-layouts: 16.8 us -> 33.2 us
  other arithmetic: 14.5 us -> 19.6 us
  blocking collectives: 34.7 us -> 30.7 us
    ppermute x0 -> x7, waiting for transfers between devices: none -> 53 us  [the longest x4 28.5 us: ring_gather(): lower.append(lax.ppermute(lower[-1] if lower else value, axis, pairs))]
    all_to_all x1, waiting for transfers between devices: 50.6 us -> 0.01 us  [side_by_side(): lax.all_to_all(both, axis, split_axis=split_dim, concat_axis=concat_dim,...]
    all_gather x1, waiting for transfers between devices: 45.8 us -> 0.01 us  [sent_together(): lax.all_gather(both, axis, axis=dim, tiled=True)]
    all_gather x1 -> x0, waiting for transfers between devices: 21 us -> none  [local(): lax.all_gather(caption_states, 'seq', axis=1, tiled=True)]
    ppermute x0 -> x7, starting transfers between devices: none -> 20.2 us  [the longest x4 11.7 us: ring_gather(): lower.append(lax.ppermute(lower[-1] if lower else value, axis, pairs))]
    unnamed x29 -> x44, local copies, waits for them, and re-layouts: 9.77 us -> 19.1 us
    reduce_scatter x1, waiting for transfers between devices: 6.91 us -> 16.1 us  [local(): lax.psum_scatter(lax.dot_general(columns, stacked, contract_rows, preferr...]
    convert_element_type x0 -> x1, other arithmetic: none -> 5.78 us  [normalize_rows(): (values * lax.rsqrt(mean_square + norm_epsilon) * caption_gain).astype(jn...]
  transfers between devices with their start and end apart: 4 -> 10, of which waited for: 4 -> 6; matrix products, arithmetic and copies ran while one was open for 15% -> 26% of each run, Pallas kernels for 0% -> 0%
where the time goes in v1:
time: 223 us; the launch traced here: 222 us
  waiting for transfers between devices  69.1 us (31%)
  local copies, waits for them, and re-layouts  33.2 us (15%)
  blocking collectives  30.7 us (14%)
  starting transfers between devices  29.8 us (13%)
  matrix products  25.1 us (11%)
  other arithmetic  19.6 us (9%)
  between operations  14.3 us (6%)
    all_to_all x1, blocking collectives, side_by_side(): lax.all_to_all(both, axis, split_axis=split_dim, concat_axis=concat_dim,...  30.7 us
    ppermute x4, waiting for transfers between devices, ring_gather(): lower.append(lax.ppermute(lower[-1] if lower else value, axis, pairs))  28.5 us
    ppermute x3, waiting for transfers between devices, ring_gather(): upper.append(lax.ppermute(upper[-1] if upper else value, axis, back))  24.5 us
    unnamed x44, local copies, waits for them, and re-layouts  19.1 us
    reduce_scatter x1, waiting for transfers between devices, local(): lax.psum_scatter(lax.dot_general(columns, stacked, contract_rows, preferr...  16.1 us
    ppermute x4, starting transfers between devices, ring_gather(): lower.append(lax.ppermute(lower[-1] if lower else value, axis, pairs))  11.7 us
    all_to_all x1, starting transfers between devices, side_by_side(): lax.all_to_all(both, axis, split_axis=split_dim, concat_axis=concat_dim,...  9.51 us
    ppermute x3, starting transfers between devices, ring_gather(): upper.append(lax.ppermute(upper[-1] if upper else value, axis, back))  8.48 us
  transfers between devices with their start and end apart: 10, of which 6 were waited for; matrix products, arithmetic and copies ran while one was open for 26% of the time, Pallas kernels for 0%

profile of v1, /device:TPU:12, one launch (start us, length us, event | category | flops | bytes accessed | tf_op | source)
XLA Modules:
  0.0 222.2 jit_solution(9378618968030740308)
XLA Ops:
  7.2 3.6 %collective-permute-start = (bf16[1,64,4096]{2,1,0:T(8,128)(2,1)}, bf16[1,64,4096]{2,1,0:T(8,128)(2,1)S(1)}, u32[]{:S(2)}, u32[]{:S(2)}) collective-permute-start(bf16[1,64,4096]{2,1,0:T(8,128)(2,1)} %param.22), channel_id=1, source_target_pairs={{0,16},{16,32},{32,48},{48,64},{64,80},{80,96},{96,112},{112,0},{1... | collective-permute-start | bytes 1572872 | tf_op jit(solution)/shard_map/ppermute | solution.py:23
  10.9 2.4 %collective-permute-start.4 = (bf16[1,64,4096]{2,1,0:T(8,128)(2,1)}, bf16[1,64,4096]{2,1,0:T(8,128)(2,1)S(1)}, u32[]{:S(2)}, u32[]{:S(2)}) collective-permute-start(bf16[1,64,4096]{2,1,0:T(8,128)(2,1)} %param.22), channel_id=1, source_target_pairs={{16,0},{32,16},{48,32},{64,48},{80,64},{96,80},{112,96},{0,112},{1... | collective-permute-start | bytes 1572872 | tf_op jit(solution)/shard_map/ppermute | solution.py:25
  13.2 9.9 %collective-permute-done = bf16[1,64,4096]{2,1,0:T(8,128)(2,1)S(1)} collective-permute-done((bf16[1,64,4096]{2,1,0:T(8,128)(2,1)}, bf16[1,64,4096]{2,1,0:T(8,128)(2,1)S(1)}, u32[]{:S(2)}, u32[]{:S(2)}) %collective-permute-start) | collective-permute-done | bytes 524320 | tf_op jit(solution)/shard_map/ppermute | solution.py:23
  23.1 3.5 %collective-permute-start.1 = (bf16[1,64,4096]{2,1,0:T(8,128)(2,1)S(1)}, bf16[1,64,4096]{2,1,0:T(8,128)(2,1)S(1)}, u32[]{:S(2)}, u32[]{:S(2)}) collective-permute-start(bf16[1,64,4096]{2,1,0:T(8,128)(2,1)S(1)} %collective-permute-done), channel_id=1, source_target_pairs={{0,16},{16,32},{32,48},{48,64},{64,80},{80,96},{96,112},{112,0},{1... | collective-permute-start | bytes 1572872 | tf_op jit(solution)/shard_map/ppermute | solution.py:23
  31.6 7.0 %collective-permute-done.1 = bf16[1,64,4096]{2,1,0:T(8,128)(2,1)S(1)} collective-permute-done((bf16[1,64,4096]{2,1,0:T(8,128)(2,1)S(1)}, bf16[1,64,4096]{2,1,0:T(8,128)(2,1)S(1)}, u32[]{:S(2)}, u32[]{:S(2)}) %collective-permute-start.1) | collective-permute-done | bytes 524320 | tf_op jit(solution)/shard_map/ppermute | solution.py:23
  38.6 2.7 %collective-permute-start.2 = (bf16[1,64,4096]{2,1,0:T(8,128)(2,1)S(1)}, bf16[1,64,4096]{2,1,0:T(8,128)(2,1)}, u32[]{:S(2)}, u32[]{:S(2)}) collective-permute-start(bf16[1,64,4096]{2,1,0:T(8,128)(2,1)S(1)} %collective-permute-done.1), channel_id=1, source_target_pairs={{0,16},{16,32},{32,48},{48,64},{64,80},{80,96},{96,112},{112,0},{1... | collective-permute-start | bytes 1572872 | tf_op jit(solution)/shard_map/ppermute | solution.py:23
  44.5 4.0 %collective-permute-start.5 = (bf16[1,64,4096]{2,1,0:T(8,128)(2,1)S(1)}, bf16[1,64,4096]{2,1,0:T(8,128)(2,1)}, u32[]{:S(2)}, u32[]{:S(2)}) collective-permute-start(bf16[1,64,4096]{2,1,0:T(8,128)(2,1)S(1)} %collective-permute-done.4), channel_id=1, source_target_pairs={{16,0},{32,16},{48,32},{64,48},{80,64},{96,80},{112,96},{0,112},{1... | collective-permute-start | bytes 1572872 | tf_op jit(solution)/shard_map/ppermute | solution.py:25
  48.5 5.5 %collective-permute-done.2 = bf16[1,64,4096]{2,1,0:T(8,128)(2,1)} collective-permute-done((bf16[1,64,4096]{2,1,0:T(8,128)(2,1)S(1)}, bf16[1,64,4096]{2,1,0:T(8,128)(2,1)}, u32[]{:S(2)}, u32[]{:S(2)}) %collective-permute-start.2) | collective-permute-done | bytes 524320 | tf_op jit(solution)/shard_map/ppermute | solution.py:23
  56.7 9.5 %all-to-all-start = ((bf16[6,128,8,128]{3,1,0,2:T(8,128)(2,1)}), bf16[6,128,8,128]{3,1,0,2:T(8,128)(2,1)S(1)}, u32[]{:S(2)}, u32[]{:S(2)}) async-start(bf16[6,128,8,128]{3,1,0,2:T(8,128)(2,1)} %copy_dynamic-update-slice_fusion), calls=%async_computation | async-start | bytes 3145728 | tf_op jit(solution)/shard_map/all_to_all | solution.py:44
  68.3 2.1 collective-permute-start.6
  70.4 6.1 %collective-permute-done.3 = bf16[1,64,4096]{2,1,0:T(8,128)(2,1)} collective-permute-done((bf16[1,64,4096]{2,1,0:T(8,128)(2,1)}, bf16[1,64,4096]{2,1,0:T(8,128)(2,1)}, u32[]{:S(2)}, u32[]{:S(2)}) %collective-permute-start.3) | collective-permute-done | bytes 524320 | tf_op jit(solution)/shard_map/ppermute | solution.py:23
  85.6 24.5 %collective-permute-done.6 = bf16[1,64,4096]{2,1,0:T(8,128)(2,1)S(1)} collective-permute-done((bf16[1,64,4096]{2,1,0:T(8,128)(2,1)}, bf16[1,64,4096]{2,1,0:T(8,128)(2,1)S(1)}, u32[]{:S(2)}, u32[]{:S(2)}) %collective-permute-start.6) | collective-permute-done | bytes 524320 | tf_op jit(solution)/shard_map/ppermute | solution.py:25
  110.9 5.0 %gather_fusion = bf16[8,64,4096]{2,1,0:T(8,128)(2,1)} fusion(bf16[8,64,4096]{2,1,0:T(8,128)(2,1)} %bitcast.25, s32[1024]{0:T(1024)S(1)} %pad_clamp_fusion), kind=kCustom, calls=%fused_computation | custom fusion | bytes 8388640 | tf_op jit(solution)/shard_map/gather | solution.py:28
  115.9 3.1 %multiply_reduce_fusion.2 = f32[8,64]{1,0:T(8,128)S(1)} fusion(bf16[8,64,4096]{2,1,0:T(8,128)(2,1)} %gather_fusion), kind=kLoop, calls=%fused_computation.67 | loop fusion | flops 6290944 | bytes 4196352 | tf_op jit(solution)/shard_map/reduce_sum | solution.py:50
  119.1 5.8 %fusion.50 = bf16[512,4096]{1,0:T(8,128)(2,1)} fusion(f32[4096]{0:T(1024)S(1)} %copy-done.13, f32[512]{0:T(512)S(1)} %rsqrt.12, bf16[8,64,4096]{2,1,0:T(8,128)(2,1)} %gather_fusion), kind=kLoop, calls=%fused_computation.66 | loop fusion | flops 8388608 | bytes 8407040 | tf_op jit(solution)/shard_map/convert_element_type | solution.py:51
  126.8 3.9 %fusion.51 = bf16[512,1,128]{2,0,1:T(8,128)(2,1)S(1)} fusion(bf16[512,4096]{1,0:T(8,128)(2,1)} %fusion.50, bf16[4096,256]{1,0:T(8,128)(2,1)} %all-gather.2.cloned.1.call-done), kind=kOutput, calls=%fused_computation.72 | convolution fusion | flops 536936448 | bytes 5373952 | tf_op jit(solution)/shard_map/dot_general | solution.py:123
  130.7 3.2 %fusion.52 = bf16[512,1,128]{2,0,1:T(8,128)(2,1)} fusion(bf16[512,4096]{1,0:T(8,128)(2,1)S(1)} %copy-done, bf16[4096,256]{1,0:T(8,128)(2,1)} %all-gather.2.cloned.1.call-done), kind=kOutput, calls=%fused_computation.73 | convolution fusion | flops 536936448 | bytes 5373952 | tf_op jit(solution)/shard_map/dot_general | solution.py:124
  134.0 7.1 %while.31 = (s32[]{:T(128)}, f32[512,1,128]{0,2,1:T(8,128)S(1)}, f32[512,1,128]{0,2,1:T(8,128)S(1)}, bf16[2,512,1,128]{3,1,2,0:T(8,128)(2,1)S(1)}, bf16[2,512,1,...) while((s32[]{:T(128)}, f32[512,1,128]{0,2,1:T(8,128)S(1)}, ...), condition=%wide.region_10.11_spmd.clone, body=%wide.region_6.10_spmd.clone.sunk | while | flops 340524032 | bytes 11689132 | solution.py:96
  141.2 4.9 %convolution_convert_fusion = bf16[4096,256]{1,0:T(8,128)(2,1)} fusion(bf16[512,4096]{1,0:T(8,128)(2,1)} %fusion.50, bf16[512,128]{0,1:T(8,128)(2,1)S(1)} %get-tuple-element.309, bf16[512,128]{0,1:T(8,128)(2,1)S(1)} %get-tuple-element.310), kind=kOutput, calls=%fused_computation.68 | convolution fusion | flops 1075314688 | bytes 6553600 | tf_op jit(solution)/shard_map/dot_general | solution.py:168
  146.2 13.7 %while.30 = (s32[]{:T(128)}, f32[1024,1,128]{0,2,1:T(8,128)S(1)}, f32[1024,1,128]{0,2,1:T(8,128)}, bf16[2,512,1,128]{3,1,2,0:T(8,128)(2,1)S(1)}, bf16[2,512,1,12...) while((s32[]{:T(128)}, f32[1024,1,128]{0,2,1:T(8,128)S(1)}, ...), condition=%wide.region_4.5_spmd.clone, body=%wide.region_0.4_spmd.clone.sunk | while | flops 685243904 | bytes 23622340 | solution.py:96
  148.0 2.5 %fusion.102 = f32[1024,1,128]{0,2,1:T(8,128)} fusion(f32[1024,1,128]{0,2,1:T(8,128)} %get-tuple-element.483, pred[]{:T(512)S(6)} %compare.13, bf16[2,512,1,128]{3,1,2,0:T(8,128)(2,1)} %get-tuple-element.499, s32[]{:T(128)} %get-tuple-element.481, f32[512,1024]{1,0:T(8,128)S(1)} %get-tuple-element.420, f32[512]{0:T(512)S(1)} %fusion.100, ...), kind=kOutput, calls=%fused_computation.11.clone.1 | convolution fusion | flops 137101312 | bytes 3282433 | tf_op jit(solution)/shard_map/while/body/eval_jaxpr/hqk,qhd->khd/dot_general | solution.py:76
  154.8 2.7 %fusion.102 = f32[1024,1,128]{0,2,1:T(8,128)} fusion(f32[1024,1,128]{0,2,1:T(8,128)} %get-tuple-element.483, pred[]{:T(512)S(6)} %compare.13, bf16[2,512,1,128]{3,1,2,0:T(8,128)(2,1)} %get-tuple-element.499, s32[]{:T(128)} %get-tuple-element.481, f32[512,1024]{1,0:T(8,128)S(1)} %get-tuple-element.420, f32[512]{0:T(512)S(1)} %fusion.100, ...), kind=kOutput, calls=%fused_computation.11.clone.1 | convolution fusion | flops 137101312 | bytes 3282433 | tf_op jit(solution)/shard_map/while/body/eval_jaxpr/hqk,qhd->khd/dot_general | solution.py:76
  163.2 30.7 %all_to_all.30 = bf16[4,1024,1,128]{3,0,2,1:T(4,128)(2,1)S(1)} all-to-all(bf16[4,1024,1,128]{3,0,2,1:T(4,128)(2,1)S(1)} %copy.77), channel_id=1, replica_groups=mesh['section'=4,'seq'=8,'dp'=16] {'seq'}, dimensions={1} | all-to-all | bytes 2097152 | tf_op jit(solution)/shard_map/all_to_all | solution.py:44
  197.6 16.1 %reduce-scatter.2.cloned.1.call-done = bf16[256,256]{1,0:T(8,128)(2,1)} async-done(((bf16[4096,256]{1,0:T(8,128)(2,1)}), bf16[256,256]{1,0:T(8,128)(2,1)}) %reduce-scatter.2.cloned.1.call-update) | async-done | bytes 131088 | tf_op jit(solution)/shard_map/reduce_scatter | solution.py:167
  (122 shorter events, 48.7 us)
Async XLA Ops:
  7.2 35.8 %copy-start.9 = (bf16[1,128,8,128]{3,2,1,0:T(8,128)(2,1)S(1)}, bf16[1,128,8,128]{3,2,1,0:T(8,128)(2,1)}, u32[]{:S(2)}) copy-start(bf16[1,128,8,128]{3,2,1,0:T(8,128)(2,1)} %param.19) | copy-start | bytes 786436
  7.2 36.6 %copy-start.10 = (bf16[1,128,8,128]{3,2,1,0:T(8,128)(2,1)S(1)}, bf16[1,128,8,128]{3,2,1,0:T(8,128)(2,1)}, u32[]{:S(2)}) copy-start(bf16[1,128,8,128]{3,2,1,0:T(8,128)(2,1)} %param.20) | copy-start | bytes 786436
  7.2 48.7 %copy-start.11 = (bf16[1,128,8,128]{3,2,1,0:T(8,128)(2,1)S(1)}, bf16[1,128,8,128]{3,2,1,0:T(8,128)(2,1)}, u32[]{:S(2)}) copy-start(bf16[1,128,8,128]{3,2,1,0:T(8,128)(2,1)} %param.21) | copy-start | bytes 786436
  7.2 119.6 %all-gather.2.cloned.1.call-start = ((), (), s32[]{:S(2)}) async-start(), calls=%async_computation.3 | async-start | bytes 2228224 | tf_op jit(solution)/shard_map/all_gather | solution.py:38
  7.2 15.9 %collective-permute-start = (bf16[1,64,4096]{2,1,0:T(8,128)(2,1)}, bf16[1,64,4096]{2,1,0:T(8,128)(2,1)S(1)}, u32[]{:S(2)}, u32[]{:S(2)}) collective-permute-start(bf16[1,64,4096]{2,1,0:T(8,128)(2,1)} %param.22), channel_id=1, source_target_pairs={{0,16},{16,32},{32,48},{48,64},{64,80},{80,96},{96,112},{112,0},{1... | collective-permute-start | bytes 1572872 | tf_op jit(solution)/shard_map/ppermute | solution.py:23
  10.9 33.7 %collective-permute-start.4 = (bf16[1,64,4096]{2,1,0:T(8,128)(2,1)}, bf16[1,64,4096]{2,1,0:T(8,128)(2,1)S(1)}, u32[]{:S(2)}, u32[]{:S(2)}) collective-permute-start(bf16[1,64,4096]{2,1,0:T(8,128)(2,1)} %param.22), channel_id=1, source_target_pairs={{16,0},{32,16},{48,32},{64,48},{80,64},{96,80},{112,96},{0,112},{1... | collective-permute-start | bytes 1572872 | tf_op jit(solution)/shard_map/ppermute | solution.py:25
  23.1 33.5 %copy-start.3 = (bf16[1,64,4096]{2,1,0:T(8,128)(2,1)}, bf16[1,64,4096]{2,1,0:T(8,128)(2,1)S(1)}, u32[]{:S(2)}) copy-start(bf16[1,64,4096]{2,1,0:T(8,128)(2,1)S(1)} %collective-permute-done) | copy-start | bytes 1572868
  23.1 15.4 %collective-permute-start.1 = (bf16[1,64,4096]{2,1,0:T(8,128)(2,1)S(1)}, bf16[1,64,4096]{2,1,0:T(8,128)(2,1)S(1)}, u32[]{:S(2)}, u32[]{:S(2)}) collective-permute-start(bf16[1,64,4096]{2,1,0:T(8,128)(2,1)S(1)} %collective-permute-done), channel_id=1, source_target_pairs={{0,16},{16,32},{32,48},{48,64},{64,80},{80,96},{96,112},{112,0},{1... | collective-permute-start | bytes 1572872 | tf_op jit(solution)/shard_map/ppermute | solution.py:23
  38.6 18.1 %copy-start.5 = (bf16[1,64,4096]{2,1,0:T(8,128)(2,1)}, bf16[1,64,4096]{2,1,0:T(8,128)(2,1)S(1)}, u32[]{:S(2)}) copy-start(bf16[1,64,4096]{2,1,0:T(8,128)(2,1)S(1)} %collective-permute-done.1) | copy-start | bytes 1572868
  38.6 15.4 %collective-permute-start.2 = (bf16[1,64,4096]{2,1,0:T(8,128)(2,1)S(1)}, bf16[1,64,4096]{2,1,0:T(8,128)(2,1)}, u32[]{:S(2)}, u32[]{:S(2)}) collective-permute-start(bf16[1,64,4096]{2,1,0:T(8,128)(2,1)S(1)} %collective-permute-done.1), channel_id=1, source_target_pairs={{0,16},{16,32},{32,48},{48,64},{64,80},{80,96},{96,112},{112,0},{1... | collective-permute-start | bytes 1572872 | tf_op jit(solution)/shard_map/ppermute | solution.py:23
  43.8 22.5 %copy-start.14 = (s32[16]{0:T(128)S(1)}, s32[16]{0:T(128)}, u32[]{:S(2)}) copy-start(s32[16]{0:T(128)} %param.26) | copy-start | bytes 196
  43.8 23.1 %copy-start.15 = (s32[16]{0:T(128)S(1)}, s32[16]{0:T(128)}, u32[]{:S(2)}) copy-start(s32[16]{0:T(128)} %param.27) | copy-start | bytes 196
  44.5 23.8 %collective-permute-start.5 = (bf16[1,64,4096]{2,1,0:T(8,128)(2,1)S(1)}, bf16[1,64,4096]{2,1,0:T(8,128)(2,1)}, u32[]{:S(2)}, u32[]{:S(2)}) collective-permute-start(bf16[1,64,4096]{2,1,0:T(8,128)(2,1)S(1)} %collective-permute-done.4), channel_id=1, source_target_pairs={{16,0},{32,16},{48,32},{64,48},{80,64},{96,80},{112,96},{0,112},{1... | collective-permute-start | bytes 1572872 | tf_op jit(solution)/shard_map/ppermute | solution.py:25
  54.0 22.5 %collective-permute-start.3 = (bf16[1,64,4096]{2,1,0:T(8,128)(2,1)}, bf16[1,64,4096]{2,1,0:T(8,128)(2,1)}, u32[]{:S(2)}, u32[]{:S(2)}) collective-permute-start(bf16[1,64,4096]{2,1,0:T(8,128)(2,1)} %collective-permute-done.2), channel_id=1, source_target_pairs={{0,16},{16,32},{32,48},{48,64},{64,80},{80,96},{96,112},{112,0},{1... | collective-permute-start | bytes 1572872 | tf_op jit(solution)/shard_map/ppermute | solution.py:23
  56.7 68.2 %all-to-all-start = ((bf16[6,128,8,128]{3,1,0,2:T(8,128)(2,1)}), bf16[6,128,8,128]{3,1,0,2:T(8,128)(2,1)S(1)}, u32[]{:S(2)}, u32[]{:S(2)}) async-start(bf16[6,128,8,128]{3,1,0,2:T(8,128)(2,1)} %copy_dynamic-update-slice_fusion), calls=%async_computation | async-start | bytes 3145728 | tf_op jit(solution)/shard_map/all_to_all | solution.py:44
  66.2 147.6 %reduce-scatter.2.cloned.1.call-start = ((), (), s32[]{:S(2)}) async-start(), calls=%async_computation.4 | async-start | bytes 2228224 | tf_op jit(solution)/shard_map/reduce_scatter | solution.py:167
  67.5 12.8 %copy-start.6 = (bf16[1,64,4096]{2,1,0:T(8,128)(2,1)S(1)}, bf16[1,64,4096]{2,1,0:T(8,128)(2,1)}, u32[]{:S(2)}) copy-start(bf16[1,64,4096]{2,1,0:T(8,128)(2,1)} %copy-done.5) | copy-start | bytes 1572868
  67.5 13.7 %copy-start.4 = (bf16[1,64,4096]{2,1,0:T(8,128)(2,1)S(1)}, bf16[1,64,4096]{2,1,0:T(8,128)(2,1)}, u32[]{:S(2)}) copy-start(bf16[1,64,4096]{2,1,0:T(8,128)(2,1)} %copy-done.3) | copy-start | bytes 1572868
  68.3 13.7 %copy-start.2 = (bf16[1,64,4096]{2,1,0:T(8,128)(2,1)S(1)}, bf16[1,64,4096]{2,1,0:T(8,128)(2,1)}, u32[]{:S(2)}) copy-start(bf16[1,64,4096]{2,1,0:T(8,128)(2,1)} %param.22) | copy-start | bytes 1572868
  68.3 41.8 %collective-permute-start.6 = (bf16[1,64,4096]{2,1,0:T(8,128)(2,1)}, bf16[1,64,4096]{2,1,0:T(8,128)(2,1)S(1)}, u32[]{:S(2)}, u32[]{:S(2)}) collective-permute-start(bf16[1,64,4096]{2,1,0:T(8,128)(2,1)} %collective-permute-done.5), channel_id=1, source_target_pairs={{16,0},{32,16},{48,32},{64,48},{80,64},{96,80},{112,96},{0,112},{1... | collective-permute-start | bytes 1572872 | tf_op jit(solution)/shard_map/ppermute | solution.py:25
  115.9 3.2 %copy-start.13 = (f32[4096]{0:T(1024)S(1)}, f32[4096]{0:T(1024)}, u32[]{:S(2)}) copy-start(f32[4096]{0:T(1024)} %param.23) | copy-start | bytes 49156
  126.8 3.9 %copy-start = (bf16[512,4096]{1,0:T(8,128)(2,1)S(1)}, bf16[512,4096]{1,0:T(8,128)(2,1)}, u32[]{:S(2)}) copy-start(bf16[512,4096]{1,0:T(8,128)(2,1)} %fusion.50) | copy-start | bytes 12582916
  130.7 3.2 %copy-start.8 = (f32[512,1,128]{0,2,1:T(8,128)S(1)}, f32[512,1,128]{0,2,1:T(8,128)}, u32[]{:S(2)}) copy-start(f32[512,1,128]{0,2,1:T(8,128)} %custom-call.3) | copy-start | bytes 786436
  141.1 5.0 %copy-start.1 = (bf16[2,512,1,128]{3,1,2,0:T(8,128)(2,1)}, bf16[2,512,1,128]{3,1,2,0:T(8,128)(2,1)S(1)}, u32[]{:S(2)}) copy-start(bf16[2,512,1,128]{3,1,2,0:T(8,128)(2,1)S(1)} %get-tuple-element.107) | copy-start | bytes 786436
  (6 other events, 12.3 us)
Sparse Core Ops, SparseCore 0:
  28.3 47.4 all-gather.1
  146.2 67.4 reduce-scatter.1
